TPU v7x, 256 devices: a whole 4x4x8 slice. The times are simulated.
256 devices in a mesh: expert: 64 (over y, z, core), tensor: 4 (over x).
Axes of the slice: x: 4, y: 4, z: 8, core: 2. Of those that a mesh axis runs over, the one named last changes fastest.
Arguments:
- attn_heads: bfloat16 [8192, 4096], P('expert', 'tensor'), may hold values from -6 to 6
- out_proj: bfloat16 [4096, 4096], P('tensor', 'expert'), may hold values from -0.09375 to 0.09375
- residual: bfloat16 [8192, 4096], P('expert'), may hold values from -6 to 6
- norm_gain: float32 [4096], replicated, may hold values from 0.1 to 1.9
- route_ids: int32 [8192, 8], P('expert'), may hold values from 0 to 63, all different within a row; in each aligned block of 128 rows (0 to 127, 128 to 255, ...) at most 18 rows name the same one
- route_weights: float32 [8192, 8], P('expert'), may hold values from 0.05 to 1
- w_gate: bfloat16 [64, 4096, 1536], P('expert', None, 'tensor'), may hold values from -0.09375 to 0.09375
- w_up: bfloat16 [64, 4096, 1536], P('expert', None, 'tensor'), may hold values from -0.09375 to 0.09375
- w_down: bfloat16 [64, 1536, 4096], P('expert', 'tensor'), may hold values from -0.15625 to 0.15625
Outputs:
- layer_out: bfloat16 [8192, 4096], P('expert', 'tensor')
Inputs may be any that keep to these rules, and one draw needn't show every extreme that they name: `route_ids`: each row names 8 different experts. In aligned blocks of 128 rows no expert is named more than 18 times, a bound that some block reaches.
All inputs are finite; a program needn't handle non-finite values.
Results may differ from a plain program's by a relative error of at most 0.015.
Values may be sent and summed in bfloat16 or wider, within the bound.
A program may use at most 128 MiB of HBM per device.

v0:
```python
import jax
import jax.numpy as jnp
from jax import lax
from jax.sharding import PartitionSpec as P

EXPERTS = 64
CAP = 18


def slot_places(ids, experts, capacity):
    row_count, top_count = ids.shape
    onehot = (ids[:, :, None] == jnp.arange(experts, dtype=jnp.int32)[None, None, :]).astype(
        jnp.int32
    )
    flattened = onehot.reshape(row_count * top_count, experts)
    before = jnp.cumsum(flattened, axis=0) - flattened
    slot_rank = jnp.sum(before * flattened, axis=1).reshape(row_count, top_count)
    return ids * capacity + slot_rank


def per_device(
    attn_heads, out_proj, residual, norm_gain, route_ids, route_weights, w_gate, w_up, w_down
):
    model_width = residual.shape[1]
    groups = lax.axis_size("expert")
    members = lax.axis_size("tensor")
    member = lax.axis_index("tensor")
    per_group = w_gate.shape[0]
    slot_count = EXPERTS * CAP
    block_cols = model_width // members
    heads_out = jnp.dot(
        attn_heads,
        lax.all_gather(out_proj, "expert", axis=1, tiled=True),
        preferred_element_type=jnp.float32,
    )
    attn_out = lax.psum(heads_out.astype(jnp.bfloat16), "tensor").astype(jnp.float32)
    hidden = residual.astype(jnp.float32) + attn_out
    normed = (
        hidden * lax.rsqrt(jnp.mean(hidden * hidden, axis=-1, keepdims=True) + 1e-06) * norm_gain
    ).astype(jnp.bfloat16)
    slot_index = slot_places(route_ids, EXPERTS, CAP)
    slot_range = jnp.arange(slot_count, dtype=jnp.int32)
    slot_hits = jnp.sum(
        (slot_index[:, :, None] == slot_range[None, None, :]).astype(jnp.bfloat16), axis=1
    )
    buffer = jnp.einsum("rj,rd->jd", slot_hits, normed, preferred_element_type=jnp.float32).astype(
        jnp.bfloat16
    )
    buffer = buffer.reshape(groups, per_group, CAP, model_width)
    arrived = lax.all_to_all(buffer, "expert", split_axis=0, concat_axis=0, tiled=True)
    gate_acc = jnp.einsum("gxcd,xdf->gxcf", arrived, w_gate, preferred_element_type=jnp.float32)
    upper = jnp.einsum("gxcd,xdf->gxcf", arrived, w_up, preferred_element_type=jnp.float32)
    activation = (jax.nn.silu(gate_acc) * upper).astype(jnp.bfloat16)
    product_term = jnp.einsum(
        "gxcf,xfd->gxcd", activation, w_down, preferred_element_type=jnp.float32
    )
    product_term = lax.optimization_barrier(product_term.astype(jnp.bfloat16)).astype(jnp.float32)
    product_term = product_term.reshape(
        groups, per_group, CAP, 1 * lax.axis_size("tensor"), block_cols
    )
    shares = lax.psum_scatter(
        jnp.transpose(product_term, (3, 0, 1, 2, 4)).astype(jnp.bfloat16),
        "tensor",
        scatter_dimension=0,
        tiled=True,
    ).astype(jnp.float32)
    expert_out = shares[0].astype(jnp.bfloat16)
    returned = lax.all_to_all(expert_out, "expert", split_axis=0, concat_axis=0, tiled=True)
    weights = route_weights / jnp.sum(route_weights, axis=-1, keepdims=True)
    picked = returned.reshape(slot_count, block_cols)[slot_index]
    mixture = jnp.sum(weights[:, :, None] * picked.astype(jnp.float32), axis=1)
    own_hidden = lax.dynamic_slice_in_dim(hidden, member * block_cols, block_cols, 1)
    return (own_hidden + mixture).astype(jnp.bfloat16)


def solution(mesh):
    placed = (
        P("expert", "tensor"),
        P("tensor", "expert"),
        P("expert", None),
        P(),
        P("expert", None),
        P("expert", None),
        P("expert", None, "tensor"),
        P("expert", None, "tensor"),
        P("expert", "tensor", None),
    )
    return jax.shard_map(
        per_device, mesh=mesh, in_specs=placed, out_specs=P("expert", "tensor"), check_vma=False
    )
```

profile of v0, /device:TPU:1, one launch (start us, length us, event | category | flops | bytes accessed | tf_op | source)
XLA Modules:
  0.0 692.8 jit_solution(6831662103066266211)
XLA Ops:
  6.5 0.7 all-gather.2.cloned.1.call-update
  7.3 90.2 %all-gather.2.cloned.1.call-done = bf16[1024,4096]{0,1:T(8,128)(2,1)} async-done(((bf16[1024,64]{0,1:T(8,128)(2,1)}), bf16[1024,4096]{0,1:T(8,128)(2,1)}) %all-gather.2.cloned.1.call-update) | async-done | bytes 8388624 | tf_op jit(solution)/shard_map/all_gather | solution.py:33
  97.5 7.4 %convolution_convert_fusion.1 = bf16[128,4096]{1,0:T(8,128)(2,1)} fusion(bf16[128,1024]{1,0:T(8,128)(2,1)} %param.9, bf16[1024,4096]{0,1:T(8,128)(2,1)} %all-gather.2.cloned.1.call-done), kind=kOutput, calls=%fused_computation.10 | convolution fusion | flops 1074266112 | bytes 9699328 | tf_op jit(solution)/shard_map/dot_general | solution.py:31
  105.0 0.1 copy.47
  105.1 0.1 eq.43
  105.3 0.7 fusion.30
  106.0 31.1 %reduce-window.6 = s32[64,8,128]{2,1,0:T(8,128)S(1)} reduce-window(s32[64,8,128]{2,1,0:T(8,128)} %fusion.30, s32[]{:T(128)} %constant.11.clone.1), window={size=1x1x128 pad=0_0x0_0x127_0}, to_apply=%region_2.0 | reduce-window | flops 8323072 | bytes 524292 | tf_op jit(solution)/shard_map/reduce-window
  137.1 0.8 slice.10
  138.0 1.1 copy.49
  139.2 0.1 broadcast_add_fusion
  139.5 0.1 copy.52
  139.7 1.5 fusion.11
  141.1 10.4 %all-reduce.2.cloned.1.call-done = bf16[128,4096]{1,0:T(8,128)(2,1)} async-done(((bf16[128,4096]{1,0:T(8,128)(2,1)}), bf16[128,4096]{1,0:T(8,128)(2,1)}) %all-reduce.2.cloned.1.call-update) | async-done | bytes 1048592 | tf_op jit(solution)/shard_map/psum | solution.py:36
  151.5 3.4 convert_add_fusion
  155.0 5.1 convolution_convert_fusion
  160.1 13.9 %reshape.76 = bf16[64,1,18,4096]{3,2,0,1:T(8,128)(2,1)} reshape(bf16[1152,4096]{1,0:T(8,128)(2,1)} %convolution_convert_fusion) | data formatting | bytes 18874368 | tf_op jit(solution)/shard_map/reshape | solution.py:49
  174.0 288.3 %all_to_all.10 = bf16[64,1,18,4096]{3,2,1,0:T(8,128)(2,1)S(1)} all-to-all(bf16[64,1,18,4096]{3,2,1,0:T(8,128)(2,1)} %bitcast.96), channel_id=1, replica_groups=mesh['expert'=64,'tensor'=4] {'expert'}, dimensions={0} | all-to-all | bytes 18874368 | tf_op jit(solution)/shard_map/all_to_all | solution.py:50
  462.3 6.2 fusion.2
  468.5 7.3 %fusion.20 = bf16[64,18,384]{2,0,1:T(8,128)(2,1)S(1)} fusion(bf16[1,4096,384]{2,1,0:T(8,128)(2,1)S(1)} %copy-done.7, bf16[64,1,18,4096]{3,2,1,0:T(8,128)(2,1)S(1)} %all_to_all.10, f32[64,18,384]{2,0,1:T(8,128)S(1)} %fusion.2), kind=kOutput, calls=%fused_computation.29 | convolution fusion | flops 3626532864 | bytes 15237120 | tf_op jit(solution)/shard_map/gxcd,xdf->gxcf/dot_general | solution.py:52
  475.9 7.5 %convert_bitcast_fusion = bf16[64,1,18,4096]{3,0,2,1:T(8,128)(2,1)} fusion(bf16[64,18,384]{2,0,1:T(8,128)(2,1)S(1)} %fusion.20, bf16[1,384,4096]{2,1,0:T(8,128)(2,1)S(1)} %copy-done), kind=kOutput, calls=%fused_computation.7 | convolution fusion | flops 3628597248 | bytes 13467648 | tf_op jit(solution)/shard_map/gxcf,xfd->gxcd/dot_general | solution.py:54
  483.3 9.0 %copy.74 = bf16[1,18,8,4,8,1024]{5,4,2,1,0,3:T(8,128)(2,1)} copy(bf16[1,18,8,4,8,1024]{5,4,3,2,1,0:T(8,128)(2,1)} %bitcast.98) | data formatting | bytes 18874368 | tf_op jit(solution)/shard_map/convert_element_type | solution.py:62
  492.3 87.7 %reduce-scatter.2.cloned.1.call-done = bf16[1,64,1,18,1024]{4,1,3,2,0:T(8,128)(2,1)} async-done(((bf16[4,64,1,18,1024]{4,1,3,2,0:T(8,128)(2,1)}), bf16[1,64,1,18,1024]{4,1,3,2,0:T(8,128)(2,1)}) %reduce-scatter.2.cloned.1.call-update) | async-done | bytes 2359312 | tf_op jit(solution)/shard_map/reduce_scatter | solution.py:61
  580.1 4.7 copy.56
  584.8 10.9 %all-to-all-start.1 = ((bf16[64,1,18,1024]{3,2,1,0:T(8,128)(2,1)}), bf16[64,1,18,1024]{3,2,1,0:T(8,128)(2,1)}, u32[]{:S(2)}, u32[]{:S(2)}) async-start(bf16[64,1,18,1024]{3,2,1,0:T(8,128)(2,1)} %copy.56), calls=%async_computation.2 | async-start | bytes 6291456 | tf_op jit(solution)/shard_map/all_to_all | solution.py:68
  595.8 0.1 copy.57
  595.9 0.1 reshape.85
  596.0 0.1 copy.46
  596.1 73.1 %all-to-all-done.1 = bf16[64,1,18,1024]{3,2,1,0:T(8,128)(2,1)} async-done(((bf16[64,1,18,1024]{3,2,1,0:T(8,128)(2,1)}), bf16[64,1,18,1024]{3,2,1,0:T(8,128)(2,1)}, u32[]{:S(2)}, u32[]{:S(2)}) %all-to-all-start.1) | async-done | bytes 2359328 | tf_op jit(solution)/shard_map/all_to_all | solution.py:68
  669.2 4.3 reshape.82
  673.5 8.0 %gather_fusion = bf16[1024,1024]{1,0:T(8,128)(2,1)} fusion(bf16[1152,1024]{1,0:T(8,128)(2,1)} %reshape.82, s32[1024]{0:T(1024)S(1)} %broadcast_clamp_fusion), kind=kCustom, calls=%fused_computation | custom fusion | bytes 4198400 | tf_op jit(solution)/shard_map/gather | solution.py:70
  681.5 2.9 fusion.7
  684.4 1.8 add_convert_fusion
  (33 shorter events, 0.6 us)
Async XLA Ops:
  6.5 469.3 %copy-start = (bf16[1,384,4096]{2,1,0:T(8,128)(2,1)S(1)}, bf16[1,384,4096]{2,1,0:T(8,128)(2,1)}, u32[]{:S(2)}) copy-start(bf16[1,384,4096]{2,1,0:T(8,128)(2,1)} %param.17) | copy-start | bytes 9437188
  6.5 90.9 %all-gather.2.cloned.1.call-start = ((), (), s32[]{:S(2)}) async-start(), calls=%async_computation.3 | async-start | bytes 8519680 | tf_op jit(solution)/shard_map/all_gather | solution.py:33
  7.3 97.7 %copy-start.4 = (s32[128,8]{0,1:T(8,128)S(1)}, s32[128,8]{0,1:T(8,128)}, u32[]{:S(2)}) copy-start(s32[128,8]{0,1:T(8,128)} %param.13) | copy-start | bytes 12292
  7.3 144.2 %all-reduce.2.cloned.1.call-start = ((), (), s32[]{:S(2)}) async-start(), calls=%async_computation.4 | async-start | bytes 2097152 | tf_op jit(solution)/shard_map/psum | solution.py:36
  104.9 475.1 %reduce-scatter.2.cloned.1.call-start = ((), (), s32[]{:S(2)}) async-start(), calls=%async_computation.5 | async-start | bytes 11796480 | tf_op jit(solution)/shard_map/reduce_scatter | solution.py:61
  137.1 17.8 %copy-start.5 = (f32[4096]{0:T(1024)S(1)}, f32[4096]{0:T(1024)}, u32[]{:S(2)}) copy-start(f32[4096]{0:T(1024)} %param.12) | copy-start | bytes 49156
  151.5 3.4 copy-start.1
  151.5 3.4 copy-start.2
  174.0 288.3 %copy-start.6 = (bf16[1,4096,384]{2,1,0:T(8,128)(2,1)S(1)}, bf16[1,4096,384]{2,1,0:T(8,128)(2,1)}, u32[]{:S(2)}) copy-start(bf16[1,4096,384]{2,1,0:T(8,128)(2,1)} %param.15) | copy-start | bytes 9437188
  462.3 6.2 copy-start.7
  584.8 11.2 %copy-start.3 = (f32[128,8]{0,1:T(8,128)S(1)}, f32[128,8]{0,1:T(8,128)}, u32[]{:S(2)}) copy-start(f32[128,8]{0,1:T(8,128)} %param.14) | copy-start | bytes 12292
  584.8 84.4 %all-to-all-start.1 = ((bf16[64,1,18,1024]{3,2,1,0:T(8,128)(2,1)}), bf16[64,1,18,1024]{3,2,1,0:T(8,128)(2,1)}, u32[]{:S(2)}, u32[]{:S(2)}) async-start(bf16[64,1,18,1024]{3,2,1,0:T(8,128)(2,1)} %copy.56), calls=%async_computation.2 | async-start | bytes 6291456 | tf_op jit(solution)/shard_map/all_to_all | solution.py:68
Sparse Core Ops, SparseCore 0:
  10.1 87.2 all-gather.1
  105.1 46.4 all-reduce.1
  492.4 87.5 reduce-scatter.1
where the time goes:
time: 695 us; the launch traced here: 693 us
  blocking collectives  288 us (41%)
  waiting for transfers between devices  262 us (38%)
  local copies, waits for them, and re-layouts  42.8 us (6%)
  other arithmetic  41.7 us (6%)
  matrix products  33.6 us (5%)
  between operations  13.3 us (2%)
  starting transfers between devices  11 us (2%)
    all_to_all x1, blocking collectives, per_device(): lax.all_to_all(buffer, 'expert', split_axis=0, concat_axis=0, tiled=True)  288 us
    all_gather x1, waiting for transfers between devices, per_device(): lax.all_gather(out_proj, 'expert', axis=1, tiled=True)  90.2 us
    reduce_scatter x1, waiting for transfers between devices, per_device(): lax.psum_scatter(jnp.transpose(product_term, (3, 0, 1, 2, 4)).astype(jnp....  87.7 us
    all_to_all x1, waiting for transfers between devices, per_device(): lax.all_to_all(expert_out, 'expert', split_axis=0, concat_axis=0, tiled=T...  73.1 us
    another operation x3, other arithmetic  31.3 us
    reshape x1, local copies, waits for them, and re-layouts, per_device(): buffer = buffer.reshape(groups, per_group, CAP, model_width)  13.9 us
  transfers between devices with their start and end apart: 4, of which 4 were waited for; matrix products, arithmetic and copies ran while one was open for 5% of the time, Pallas kernels for 0%

commit v1 on v0

--- a/solution.py
+++ b/solution.py
@@ -2,6 +2,7 @@
 import jax.numpy as jnp
 from jax import lax
 from jax.sharding import PartitionSpec as P
+from jax.lax import all_to_all, axis_size
 
 EXPERTS = 64
 CAP = 18
@@ -28,11 +29,11 @@
     per_group = w_gate.shape[0]
     slot_count = EXPERTS * CAP
     block_cols = model_width // members
-    heads_out = jnp.dot(
-        attn_heads,
-        lax.all_gather(out_proj, "expert", axis=1, tiled=True),
-        preferred_element_type=jnp.float32,
+    _trace_map = lambda patch, dim_i: jnp.concatenate(
+        all_to_all(jnp.stack([patch for _ in range(axis_size("expert"))], axis=0), "expert", 0, 0),
+        axis=dim_i,
     )
+    heads_out = jnp.dot(attn_heads, _trace_map(out_proj, 1), preferred_element_type=jnp.float32)
     attn_out = lax.psum(heads_out.astype(jnp.bfloat16), "tensor").astype(jnp.float32)
     hidden = residual.astype(jnp.float32) + attn_out
     normed = (

time: 695 us -> 802 us (1.15)
  blocking collectives: 288 us -> 487 us
  waiting for transfers between devices: 262 us -> 171 us
    all_to_all x0 -> x1, blocking collectives: none -> 199 us  [per_device(): all_to_all(jnp.stack([patch for _ in range(axis_size('expert'))], axis=0)...]
    all_gather x1 -> x0, waiting for transfers between devices: 90.2 us -> none  [per_device(): lax.all_gather(out_proj, 'expert', axis=1, tiled=True)]
  transfers between devices with their start and end apart: 4 -> 3, of which waited for: 4 -> 3; matrix products, arithmetic and copies ran while one was open for 5% -> 5% of each run, Pallas kernels for 0% -> 0%
where the time goes in v1:
time: 802 us; the launch traced here: 799 us
  blocking collectives  487 us (61%)
  waiting for transfers between devices  171 us (21%)
  local copies, waits for them, and re-layouts  44.9 us (6%)
  other arithmetic  41.7 us (5%)
  matrix products  30 us (4%)
  between operations  13.6 us (2%)
  starting transfers between devices  11 us (1%)
    all_to_all x1, blocking collectives, per_device(): lax.all_to_all(buffer, 'expert', split_axis=0, concat_axis=0, tiled=True)  288 us
    all_to_all x1, blocking collectives, per_device(): all_to_all(jnp.stack([patch for _ in range(axis_size('expert'))], axis=0)...  199 us
    reduce_scatter x1, waiting for transfers between devices, per_device(): lax.psum_scatter(jnp.transpose(product_term, (3, 0, 1, 2, 4)).astype(jnp....  87.8 us
    all_to_all x1, waiting for transfers between devices, per_device(): lax.all_to_all(expert_out, 'expert', split_axis=0, concat_axis=0, tiled=T...  73.1 us
    another operation x3, other arithmetic  31.3 us
  transfers between devices with their start and end apart: 3, of which 3 were waited for; matrix products, arithmetic and copies ran while one was open for 5% of the time, Pallas kernels for 0%

profile of v1, /device:TPU:1, one launch (start us, length us, event | category | flops | bytes accessed | tf_op | source)
XLA Modules:
  0.0 799.5 jit_solution(13390582816836613498)
XLA Ops:
  6.5 2.1 stack.2
  8.7 199.2 %all_to_all.15 = bf16[64,1024,64]{1,2,0:T(8,128)(2,1)S(1)} all-to-all(bf16[64,1024,64]{1,2,0:T(8,128)(2,1)S(1)} %stack.2), channel_id=1, replica_groups=mesh['expert'=64,'tensor'=4] {'expert'}, dimensions={0} | all-to-all | bytes 16777216 | tf_op jit(solution)/shard_map/all_to_all | solution.py:33
  207.8 3.9 convolution_convert_fusion.1
  211.8 0.1 copy.48
  211.9 0.1 eq.43
  212.1 0.7 fusion.30
  212.8 31.1 %reduce-window.6 = s32[64,8,128]{2,1,0:T(8,128)S(1)} reduce-window(s32[64,8,128]{2,1,0:T(8,128)} %fusion.30, s32[]{:T(128)} %constant.11.clone.1), window={size=1x1x128 pad=0_0x0_0x127_0}, to_apply=%region_2.0 | reduce-window | flops 8323072 | bytes 524292 | tf_op jit(solution)/shard_map/reduce-window
  243.9 0.8 slice.10
  244.8 1.1 copy.50
  246.0 0.1 broadcast_add_fusion
  246.3 0.1 copy.53
  246.5 1.5 fusion.11
  247.9 10.0 %all-reduce.2.cloned.1.call-done = bf16[128,4096]{1,0:T(8,128)(2,1)} async-done(((bf16[128,4096]{1,0:T(8,128)(2,1)}), bf16[128,4096]{1,0:T(8,128)(2,1)}) %all-reduce.2.cloned.1.call-update) | async-done | bytes 1048592 | tf_op jit(solution)/shard_map/psum | solution.py:37
  257.9 3.4 convert_add_fusion
  261.3 5.1 convolution_convert_fusion
  266.5 13.9 %reshape.86 = bf16[64,1,18,4096]{3,2,0,1:T(8,128)(2,1)} reshape(bf16[1152,4096]{1,0:T(8,128)(2,1)} %convolution_convert_fusion) | data formatting | bytes 18874368 | tf_op jit(solution)/shard_map/reshape | solution.py:50
  280.4 288.3 %all_to_all.16 = bf16[64,1,18,4096]{3,2,1,0:T(8,128)(2,1)S(1)} all-to-all(bf16[64,1,18,4096]{3,2,1,0:T(8,128)(2,1)} %bitcast.99), channel_id=1, replica_groups=mesh['expert'=64,'tensor'=4] {'expert'}, dimensions={0} | all-to-all | bytes 18874368 | tf_op jit(solution)/shard_map/all_to_all | solution.py:51
  568.7 6.2 fusion.2
  574.9 7.3 fusion.20
  582.2 7.5 convert_bitcast_fusion
  589.7 9.0 %copy.75 = bf16[1,18,8,4,8,1024]{5,4,2,1,0,3:T(8,128)(2,1)} copy(bf16[1,18,8,4,8,1024]{5,4,3,2,1,0:T(8,128)(2,1)} %bitcast.102) | data formatting | bytes 18874368 | tf_op jit(solution)/shard_map/convert_element_type | solution.py:63
  598.7 87.8 %reduce-scatter.2.cloned.1.call-done = bf16[1,64,1,18,1024]{4,1,3,2,0:T(8,128)(2,1)} async-done(((bf16[4,64,1,18,1024]{4,1,3,2,0:T(8,128)(2,1)}), bf16[1,64,1,18,1024]{4,1,3,2,0:T(8,128)(2,1)}) %reduce-scatter.2.cloned.1.call-update) | async-done | bytes 2359312 | tf_op jit(solution)/shard_map/reduce_scatter | solution.py:62
  686.4 4.7 copy.57
  691.2 11.0 %all-to-all-start.2 = ((bf16[64,1,18,1024]{3,2,1,0:T(8,128)(2,1)}), bf16[64,1,18,1024]{3,2,1,0:T(8,128)(2,1)}, u32[]{:S(2)}, u32[]{:S(2)}) async-start(bf16[64,1,18,1024]{3,2,1,0:T(8,128)(2,1)} %copy.57), calls=%async_computation.3 | async-start | bytes 6291456 | tf_op jit(solution)/shard_map/all_to_all | solution.py:69
  702.1 0.1 copy.58
  702.2 0.1 reshape.95
  702.4 0.1 copy.47
  702.5 73.1 %all-to-all-done.2 = bf16[64,1,18,1024]{3,2,1,0:T(8,128)(2,1)} async-done(((bf16[64,1,18,1024]{3,2,1,0:T(8,128)(2,1)}), bf16[64,1,18,1024]{3,2,1,0:T(8,128)(2,1)}, u32[]{:S(2)}, u32[]{:S(2)}) %all-to-all-start.2) | async-done | bytes 2359328 | tf_op jit(solution)/shard_map/all_to_all | solution.py:69
  775.6 4.3 reshape.92
  779.9 8.0 %gather_fusion = bf16[1024,1024]{1,0:T(8,128)(2,1)} fusion(bf16[1152,1024]{1,0:T(8,128)(2,1)} %reshape.92, s32[1024]{0:T(1024)S(1)} %broadcast_clamp_fusion), kind=kCustom, calls=%fused_computation | custom fusion | bytes 4198400 | tf_op jit(solution)/shard_map/gather | solution.py:71
  787.9 2.9 fusion.7
  790.8 1.8 add_convert_fusion
  (34 shorter events, 0.6 us)
Async XLA Ops:
  6.5 575.7 %copy-start = (bf16[1,384,4096]{2,1,0:T(8,128)(2,1)S(1)}, bf16[1,384,4096]{2,1,0:T(8,128)(2,1)}, u32[]{:S(2)}) copy-start(bf16[1,384,4096]{2,1,0:T(8,128)(2,1)} %param.17) | copy-start | bytes 9437188
  6.5 251.4 %all-reduce.2.cloned.1.call-start = ((), (), s32[]{:S(2)}) async-start(), calls=%async_computation.4 | async-start | bytes 2097152 | tf_op jit(solution)/shard_map/psum | solution.py:37
  8.7 199.2 %copy-start.3 = (bf16[128,1024]{1,0:T(8,128)(2,1)S(1)}, bf16[128,1024]{1,0:T(8,128)(2,1)}, u32[]{:S(2)}) copy-start(bf16[128,1024]{1,0:T(8,128)(2,1)} %param.9) | copy-start | bytes 786436
  207.8 4.0 copy-start.5
  211.7 474.7 %reduce-scatter.2.cloned.1.call-start = ((), (), s32[]{:S(2)}) async-start(), calls=%async_computation.5 | async-start | bytes 11796480 | tf_op jit(solution)/shard_map/reduce_scatter | solution.py:62
  243.9 17.4 %copy-start.6 = (f32[4096]{0:T(1024)S(1)}, f32[4096]{0:T(1024)}, u32[]{:S(2)}) copy-start(f32[4096]{0:T(1024)} %param.12) | copy-start | bytes 49156
  257.9 3.4 copy-start.1
  257.9 3.4 copy-start.2
  280.4 288.3 %copy-start.7 = (bf16[1,4096,384]{2,1,0:T(8,128)(2,1)S(1)}, bf16[1,4096,384]{2,1,0:T(8,128)(2,1)}, u32[]{:S(2)}) copy-start(bf16[1,4096,384]{2,1,0:T(8,128)(2,1)} %param.15) | copy-start | bytes 9437188
  568.7 6.2 copy-start.8
  691.2 11.2 %copy-start.4 = (f32[128,8]{0,1:T(8,128)S(1)}, f32[128,8]{0,1:T(8,128)}, u32[]{:S(2)}) copy-start(f32[128,8]{0,1:T(8,128)} %param.14) | copy-start | bytes 12292
  691.2 84.4 %all-to-all-start.2 = ((bf16[64,1,18,1024]{3,2,1,0:T(8,128)(2,1)}), bf16[64,1,18,1024]{3,2,1,0:T(8,128)(2,1)}, u32[]{:S(2)}, u32[]{:S(2)}) async-start(bf16[64,1,18,1024]{3,2,1,0:T(8,128)(2,1)} %copy.57), calls=%async_computation.3 | async-start | bytes 6291456 | tf_op jit(solution)/shard_map/all_to_all | solution.py:69
Sparse Core Ops, SparseCore 0:
  211.9 45.9 all-reduce.1
  598.8 87.5 reduce-scatter.1
